TPU v7x, 128 devices: a whole 4x4x4 slice. The times are simulated.
128 devices in a mesh: group: 8 (over z, core), pair: 16 (over y, x).
Axes of the slice: x: 4, y: 4, z: 4, core: 2. Of those that a mesh axis runs over, the one named last changes fastest.
Arguments:
- query_embed: bfloat16 [8, 16, 1024], P('group'), may hold values from -6 to 6
- teacher_scores: float32 [8, 16, 16, 32], P('group', 'pair'), may hold values from -9 to 9
- pair_owner: int32 [8, 16, 16, 32, 1], P('group', 'pair'), may hold values from 0 to 127; in each aligned block of 512 rows (0 to 511, 512 to 1023, ..., all dimensions but the last counted through in order) at most 8 rows name the same one
- pair_row: int32 [8, 16, 16, 32], P('group', 'pair'), may hold values from 0 to 2047
- passage_hidden: bfloat16 [262144, 1024], P(('group', 'pair')), may hold values from -24 to 24
- projection: bfloat16 [1024, 1024], replicated, may hold values from -0.1875 to 0.1875
Outputs:
- query_loss: float32 [8, 16], P('group', 'pair')
- query_grad: float32 [8, 16, 1024], P('group', 'pair')
- hidden_grad: bfloat16 [262144, 1024], P(('group', 'pair'))
- projection_grad: float32 [1024, 1024], P(('group', 'pair'))
Inputs may be any that keep to these rules, and one draw needn't show every extreme that they name: `pair_owner`: owners are numbered with group as the slower index. Among the 512 candidates held by one device, at most 8 name the same owner, and every draw has a device and an owner with exactly 8. `pair_row`: A passage may be named by several candidates.
All inputs are finite; a program needn't handle non-finite values.
Results may differ from a plain program's by a relative error of at most 0.022.
Values may be sent and summed in bfloat16 or wider, within the bound.
A program may use at most 128 MiB of HBM per device.

v0:
```python
import math
import jax
import jax.numpy as jnp
from jax import lax
from jax.sharding import PartitionSpec as P

loss_scale = 1024.0
f32, bf16, i32 = (jnp.float32, jnp.bfloat16, jnp.int32)


def iota(shape, dim):
    return lax.broadcasted_iota(i32, shape, dim)


def dot(a, b, ca, cb):
    return lax.dot_general(a, b, (((ca,), (cb,)), ((), ())), preferred_element_type=f32)


def halves(x):
    high = x.astype(bf16)
    return (high, (x - high.astype(f32)).astype(bf16))


def shards(query_embed, teacher_scores, pair_owner, pair_row, passage_hidden, projection):
    width = query_embed.shape[2]
    q_rows = query_embed.shape[1]
    cand = teacher_scores.shape[3]
    n_pair, n_group = (lax.axis_size("pair"), lax.axis_size("group"))
    n_dev = n_pair * n_group
    cap = max(2, 2 * q_rows * cand // n_dev)
    slots = n_pair * cap
    k_all = cand * n_pair
    queries_n = n_group * q_rows
    rows = passage_hidden.shape[0]
    den = float(k_all * (k_all * k_all - 1))
    inv_root = 1.0 / math.sqrt(width)
    r = lax.axis_index("pair")
    owner = pair_owner.reshape(1, q_rows * cand)
    row = pair_row.reshape(1, q_rows * cand)
    n_own = q_rows * cand
    lane = iota((1, n_own), 1)
    owner_hot = iota((n_dev, n_own), 0) == owner
    owner_b = owner_hot.astype(bf16)
    before = (iota((n_own, n_own), 0) < iota((n_own, n_own), 1)).astype(bf16)
    seen = dot(owner_b, before, 1, 0)
    slot = jnp.sum(jnp.where(owner_hot, seen, 0.0), axis=0, keepdims=True).astype(i32)
    at_slot = iota((slots, n_own), 0) == slot + r * cap
    high = (row >> 4) + 1
    low = (row & 15) * 16 + lane // cand
    req = dot(owner_b, jnp.where(at_slot, high, 0).astype(bf16), 1, 1) * 256.0 + dot(
        owner_b, jnp.where(at_slot, low, 0).astype(bf16), 1, 1
    )
    q_all = lax.all_gather(query_embed[0], "group", axis=0, tiled=True)
    got = lax.all_to_all(req, ("group", "pair"), split_axis=0, concat_axis=0, tiled=True)
    packed = got.reshape(n_group, n_pair, slots).sum(1).reshape(1, n_group * slots).astype(i32)
    pq = dot(q_all, projection, 1, 1).astype(bf16)
    s_t = dot(pq, passage_hidden, 1, 1) * inv_root
    s_hi, s_lo = halves(s_t)
    place = (iota((rows, n_group * slots), 0) == (packed >> 4) - 16).astype(bf16)
    z = dot(s_hi, place, 1, 0) + dot(s_lo, place, 1, 0)
    slot_query = (packed & 15) + q_rows * (iota((1, n_group * slots), 1) // slots)
    slot_score = jnp.sum(
        jnp.where(iota((queries_n, n_group * slots), 0) == slot_query, z, 0.0), axis=0
    ).reshape(n_group, 1, slots)
    to_send = jnp.broadcast_to(slot_score, (n_group, n_pair, slots)).reshape(n_dev, slots)
    table = lax.all_to_all(to_send, ("group", "pair"), split_axis=0, concat_axis=0, tiled=True)
    tags = (owner * cap + slot).reshape(q_rows, cand)
    tags_k = lax.all_to_all(tags, "pair", split_axis=0, concat_axis=0, tiled=True).reshape(1, k_all)
    teach_k = lax.all_to_all(
        teacher_scores.reshape(q_rows, cand), "pair", split_axis=0, concat_axis=0, tiled=True
    ).reshape(1, k_all)
    k_owner = (iota((n_dev, k_all), 0) == tags_k // cap).astype(bf16)
    k_slot = (iota((slots, k_all), 0) == tags_k % cap + cap * (iota((1, k_all), 1) // cand)).astype(
        f32
    )
    t_hi, t_lo = halves(table.T)
    picked = dot(t_hi, k_owner, 1, 0) + dot(t_lo, k_owner, 1, 0)
    s_k = jnp.sum(picked * k_slot, axis=0, keepdims=True)
    tanh_s = jnp.tanh(s_k.T - s_k)
    tanh_t = jnp.tanh(teach_k.T - teach_k)
    gap = 0.5 * (jnp.sum(tanh_s, 0, keepdims=True) - jnp.sum(tanh_t, 0, keepdims=True))
    loss = 6.0 * jnp.sum(gap * gap, axis=1, keepdims=True) / den
    grad = loss_scale * 12.0 * gap / den
    s_grad = 0.5 * jnp.sum((grad.T - grad) * (1.0 - tanh_s * tanh_s), axis=0, keepdims=True)
    values = dot(k_owner, (k_slot * s_grad).astype(bf16), 1, 1)
    back = lax.all_to_all(values, ("group", "pair"), split_axis=0, concat_axis=0, tiled=True)
    same_group = (
        iota((queries_n, n_group * slots), 0) // q_rows
        == iota((queries_n, n_group * slots), 1) // slots
    )
    spread = jnp.where(same_group, jnp.tile(back, (1, n_group)), 0.0).astype(bf16)
    w_t = dot(place, spread, 1, 1).astype(bf16)
    hidden_grad = (dot(w_t, pq, 1, 0) * inv_root).astype(bf16)
    u_part = dot(w_t, passage_hidden, 0, 0).astype(bf16)
    u_rows = lax.all_to_all(u_part, ("group", "pair"), split_axis=0, concat_axis=0, tiled=True)
    u_cols = lax.all_to_all(u_part.T, ("group", "pair"), split_axis=0, concat_axis=0, tiled=True)
    u_row = jnp.sum(u_rows.astype(f32), 0, keepdims=True) * inv_root
    u_col = jnp.sum(u_cols.astype(f32).reshape(n_dev, width // n_dev, queries_n), 0) * inv_root
    r_hi, r_lo = halves(u_row)
    c_hi, c_lo = halves(u_col)
    query_grad = dot(r_hi, projection, 1, 0) + dot(r_lo, projection, 1, 0)
    projection_grad = dot(c_hi, q_all, 1, 0) + dot(c_lo, q_all, 1, 0)
    return (loss, query_grad.reshape(1, 1, width), hidden_grad, projection_grad)


def solution(mesh):
    placed = (
        P("group", None, None),
        P("group", "pair", None, None),
        P("group", "pair", None, None, None),
        P("group", "pair", None, None),
        P(("group", "pair"), None),
        P(),
    )
    return jax.shard_map(
        shards,
        mesh=mesh,
        in_specs=placed,
        out_specs=(
            P("group", "pair"),
            P("group", "pair", None),
            P(("group", "pair"), None),
            P(("group", "pair"), None),
        ),
        check_vma=False,
    )
```

profile of v0, /device:TPU:1, one launch (start us, length us, event | category | flops | bytes accessed | tf_op | source)
XLA Modules:
  0.0 141.7 jit_solution(1238981770986733830)
XLA Ops:
  0.6 0.8 broadcast_multiply_fusion
  2.0 1.4 reduce.11
  4.4 7.6 %all-to-all-start = ((s32[16,1,32]{2,1,0:T(1,128)}), s32[16,1,32]{2,1,0:T(1,128)S(1)}, u32[]{:S(2)}, u32[]{:S(2)}) async-start(s32[16,1,32]{2,1,0:T(1,128)} %add.119), calls=%async_computation | async-start | bytes 16384 | tf_op jit(solution)/shard_map/all_to_all | solution.py:68
  12.9 15.0 %all-gather = bf16[1,128,1024]{2,1,0:T(8,128)(2,1)S(1)} all-gather(bf16[1,16,1024]{2,1,0:T(8,128)(2,1)} %param.6), channel_id=2, replica_groups=mesh['group'=8,'pair'=16] {'group'}, dimensions={1}, use_global_device_ids=true | all-gather | bytes 294912 | tf_op jit(solution)/shard_map/all_gather | solution.py:53
  29.8 4.7 %convolution_multiply_fusion = f32[128,2048]{1,0:T(8,128)} fusion(bf16[128,1024]{1,0:T(8,128)(2,1)S(1)} %convolution_convert_fusion, bf16[2048,1024]{1,0:T(8,128)(2,1)} %param.10), kind=kOutput, calls=%fused_computation.8 | convolution fusion | flops 537133056 | bytes 5505024 | tf_op jit(solution)/shard_map/dot_general | solution.py:16
  34.5 6.9 %all-to-all-start.3 = ((f32[16,1,32]{2,1,0:T(1,128)}), f32[16,1,32]{2,1,0:T(1,128)S(1)}, u32[]{:S(2)}, u32[]{:S(2)}) async-start(f32[16,1,32]{2,1,0:T(1,128)} %bitcast.13), calls=%async_computation.3 | async-start | bytes 16384 | tf_op jit(solution)/shard_map/all_to_all | solution.py:69
  42.2 5.6 %all-to-all-done.3 = f32[16,1,32]{2,1,0:T(1,128)S(1)} async-done(((f32[16,1,32]{2,1,0:T(1,128)}), f32[16,1,32]{2,1,0:T(1,128)S(1)}, u32[]{:S(2)}, u32[]{:S(2)}) %all-to-all-start.3) | async-done | bytes 2080 | tf_op jit(solution)/shard_map/all_to_all | solution.py:69
  47.7 6.5 %all-to-all-start.1 = ((f32[128,1,128]{2,1,0:T(1,128)}), f32[128,1,128]{2,1,0:T(1,128)S(1)}, u32[]{:S(2)}, u32[]{:S(2)}) async-start(f32[128,1,128]{2,1,0:T(1,128)} %bitcast.3), calls=%async_computation.1 | async-start | bytes 131072 | tf_op jit(solution)/shard_map/all_to_all | solution.py:54
  55.6 8.3 %all-to-all-done.1 = f32[128,1,128]{2,1,0:T(1,128)S(1)} async-done(((f32[128,1,128]{2,1,0:T(1,128)}), f32[128,1,128]{2,1,0:T(1,128)S(1)}, u32[]{:S(2)}, u32[]{:S(2)}) %all-to-all-start.1) | async-done | bytes 65568 | tf_op jit(solution)/shard_map/all_to_all | solution.py:54
  63.9 3.3 %fusion.1 = f32[128,1024]{1,0:T(8,128)S(1)} fusion(s32[1024]{0:T(1024)S(1)} %add_bitcast_fusion, f32[128,2048]{1,0:T(8,128)} %convolution_multiply_fusion), kind=kOutput, calls=%fused_computation.3 | convolution fusion | flops 540016640 | bytes 1576960 | tf_op jit(solution)/shard_map/dot_general | solution.py:16
  67.3 1.8 %fusion.9 = f32[1024]{0:T(1024)S(1)} fusion(f32[128,1024]{1,0:T(8,128)S(1)} %fusion.1, s32[1024]{0:T(1024)S(1)} %add_bitcast_fusion, f32[128,2048]{1,0:T(8,128)S(1)} %copy-done.2, s32[1024]{0:T(1024)S(1)} %bitcast_add_fusion), kind=kOutput, calls=%fused_computation.15 | convolution fusion | flops 539753472 | bytes 1585152 | tf_op jit(solution)/shard_map/dot_general | solution.py:16
  69.7 4.5 %all-to-all-start.2 = ((f32[128,1,128]{2,1,0:T(1,128)}), f32[128,1,128]{2,1,0:T(1,128)S(1)}, u32[]{:S(2)}, u32[]{:S(2)}) async-start(f32[128,1,128]{2,1,0:T(1,128)} %bitcast.9), calls=%async_computation.2 | async-start | bytes 131072 | tf_op jit(solution)/shard_map/all_to_all | solution.py:66
  74.4 9.3 %all-to-all-done.2 = f32[128,1,128]{2,1,0:T(1,128)S(1)} async-done(((f32[128,1,128]{2,1,0:T(1,128)}), f32[128,1,128]{2,1,0:T(1,128)S(1)}, u32[]{:S(2)}, u32[]{:S(2)}) %all-to-all-start.2) | async-done | bytes 65568 | tf_op jit(solution)/shard_map/all_to_all | solution.py:66
  86.1 4.5 %all-to-all-start.4 = ((f32[128,1,128]{2,1,0:T(1,128)}), f32[128,1,128]{2,1,0:T(1,128)S(1)}, u32[]{:S(2)}, u32[]{:S(2)}) async-start(f32[128,1,128]{2,1,0:T(1,128)} %bitcast.16), calls=%async_computation.4 | async-start | bytes 131072 | tf_op jit(solution)/shard_map/all_to_all | solution.py:86
  91.3 8.9 %all-to-all-done.4 = f32[128,1,128]{2,1,0:T(1,128)S(1)} async-done(((f32[128,1,128]{2,1,0:T(1,128)}), f32[128,1,128]{2,1,0:T(1,128)S(1)}, u32[]{:S(2)}, u32[]{:S(2)}) %all-to-all-start.4) | async-done | bytes 65568 | tf_op jit(solution)/shard_map/all_to_all | solution.py:86
  100.2 1.6 %fusion.6 = bf16[2048,128]{1,0:T(8,128)(2,1)S(1)} fusion(s32[1024]{0:T(1024)S(1)} %add_bitcast_fusion, bf16[16,8,8,128]{3,2,1,0:T(8,128)(2,1)S(1)} %bitcast.62, s32[1024]{0:T(1024)S(1)} %get-tuple-element.14, s32[1024]{0:T(1024)S(1)} %get-tuple-element.15, s32[128]{0:T(128)S(1)} %get-tuple-element.16, s32[128]{0:T(128)S(1)} %get-tuple-element.17, ...), kind=kOutput, calls=%fused_computation.9 | convolution fusion | flops 539754496 | bytes 800896 | tf_op jit(solution)/shard_map/dot_general | solution.py:16
  103.6 1.5 %reduce.14 = bf16[128,1024]{1,0:T(8,128)(2,1)} reduce(bf16[128,1,1024]{2,0,1:T(8,128)(2,1)S(1)} %bitcast.58, bf16[]{:T(256)} %broadcast.377), dimensions={1}, to_apply=%copy.19.reduce_sub_computation | reduce | bytes 524290 | tf_op jit(solution)/shard_map/all_to_all | solution.py:95
  105.1 1.8 %reshape.398 = bf16[128,2,512]{2,1,0:T(2,128)(2,1)} reshape(bf16[128,1024]{1,0:T(8,128)(2,1)} %reduce.14) | data formatting | bytes 524288
  106.9 5.4 %all-to-all-start.5 = ((bf16[128,2,512]{2,1,0:T(2,128)(2,1)}), bf16[128,2,512]{2,1,0:T(2,128)(2,1)}, u32[]{:S(2)}, u32[]{:S(2)}) async-start(bf16[128,2,512]{2,1,0:T(2,128)(2,1)} %reshape.398), calls=%async_computation.5 | async-start | bytes 524288 | tf_op jit(solution)/shard_map/all_to_all | solution.py:95
  113.2 3.3 %multiply_convert_fusion = bf16[2048,1024]{1,0:T(8,128)(2,1)} fusion(bf16[2048,128]{1,0:T(8,128)(2,1)S(1)} %fusion.6, bf16[128,1024]{1,0:T(8,128)(2,1)S(1)} %convolution_convert_fusion), kind=kOutput, calls=%fused_computation | convolution fusion | flops 541065216 | bytes 4980736 | tf_op jit(solution)/shard_map/dot_general | solution.py:16
  116.4 7.0 %all-to-all-done.5 = bf16[128,2,512]{2,1,0:T(2,128)(2,1)} async-done(((bf16[128,2,512]{2,1,0:T(2,128)(2,1)}), bf16[128,2,512]{2,1,0:T(2,128)(2,1)}, u32[]{:S(2)}, u32[]{:S(2)}) %all-to-all-start.5) | async-done | bytes 262176 | tf_op jit(solution)/shard_map/all_to_all | solution.py:95
  123.4 4.2 %all-to-all-start.6 = ((bf16[128,8,128]{2,1,0:T(8,128)(2,1)}), bf16[128,8,128]{2,1,0:T(8,128)(2,1)S(1)}, u32[]{:S(2)}, u32[]{:S(2)}) async-start(bf16[128,8,128]{2,1,0:T(8,128)(2,1)} %bitcast.23), calls=%async_computation.6 | async-start | bytes 524288 | tf_op jit(solution)/shard_map/all_to_all | solution.py:96
  127.6 2.2 %reshape.399 = bf16[128,1,1024]{2,1,0:T(2,128)(2,1)S(1)} reshape(bf16[128,2,512]{2,1,0:T(2,128)(2,1)} %all-to-all-done.5) | data formatting | bytes 524288
  131.0 7.9 %all-to-all-done.6 = bf16[128,8,128]{2,1,0:T(8,128)(2,1)S(1)} async-done(((bf16[128,8,128]{2,1,0:T(8,128)(2,1)}), bf16[128,8,128]{2,1,0:T(8,128)(2,1)S(1)}, u32[]{:S(2)}, u32[]{:S(2)}) %all-to-all-start.6) | async-done | bytes 262176 | tf_op jit(solution)/shard_map/all_to_all | solution.py:96
  (56 shorter events, 15.2 us)
Async XLA Ops:
  0.6 28.3 %copy-start = (bf16[1024,1024]{1,0:T(8,128)(2,1)S(1)}, bf16[1024,1024]{1,0:T(8,128)(2,1)}, u32[]{:S(2)}) copy-start(bf16[1024,1024]{1,0:T(8,128)(2,1)} %param.11) | copy-start | bytes 6291460
  4.4 30.0 %all-to-all-start = ((s32[16,1,32]{2,1,0:T(1,128)}), s32[16,1,32]{2,1,0:T(1,128)S(1)}, u32[]{:S(2)}, u32[]{:S(2)}) async-start(s32[16,1,32]{2,1,0:T(1,128)} %add.119), calls=%async_computation | async-start | bytes 16384 | tf_op jit(solution)/shard_map/all_to_all | solution.py:68
  34.5 13.3 %all-to-all-start.3 = ((f32[16,1,32]{2,1,0:T(1,128)}), f32[16,1,32]{2,1,0:T(1,128)S(1)}, u32[]{:S(2)}, u32[]{:S(2)}) async-start(f32[16,1,32]{2,1,0:T(1,128)} %bitcast.13), calls=%async_computation.3 | async-start | bytes 16384 | tf_op jit(solution)/shard_map/all_to_all | solution.py:69
  47.7 16.1 %all-to-all-start.1 = ((f32[128,1,128]{2,1,0:T(1,128)}), f32[128,1,128]{2,1,0:T(1,128)S(1)}, u32[]{:S(2)}, u32[]{:S(2)}) async-start(f32[128,1,128]{2,1,0:T(1,128)} %bitcast.3), calls=%async_computation.1 | async-start | bytes 131072 | tf_op jit(solution)/shard_map/all_to_all | solution.py:54
  63.9 3.4 %copy-start.2 = (f32[128,2048]{1,0:T(8,128)S(1)}, f32[128,2048]{1,0:T(8,128)}, u32[]{:S(2)}) copy-start(f32[128,2048]{1,0:T(8,128)} %convolution_multiply_fusion) | copy-start | bytes 3145732
  69.7 14.0 %all-to-all-start.2 = ((f32[128,1,128]{2,1,0:T(1,128)}), f32[128,1,128]{2,1,0:T(1,128)S(1)}, u32[]{:S(2)}, u32[]{:S(2)}) async-start(f32[128,1,128]{2,1,0:T(1,128)} %bitcast.9), calls=%async_computation.2 | async-start | bytes 131072 | tf_op jit(solution)/shard_map/all_to_all | solution.py:66
  86.1 14.0 %all-to-all-start.4 = ((f32[128,1,128]{2,1,0:T(1,128)}), f32[128,1,128]{2,1,0:T(1,128)S(1)}, u32[]{:S(2)}, u32[]{:S(2)}) async-start(f32[128,1,128]{2,1,0:T(1,128)} %bitcast.16), calls=%async_computation.4 | async-start | bytes 131072 | tf_op jit(solution)/shard_map/all_to_all | solution.py:86
  100.2 2.2 %copy-start.1 = (bf16[2048,1024]{1,0:T(8,128)(2,1)S(1)}, bf16[2048,1024]{1,0:T(8,128)(2,1)}, u32[]{:S(2)}) copy-start(bf16[2048,1024]{1,0:T(8,128)(2,1)} %param.10) | copy-start | bytes 12582916
  106.9 16.5 %all-to-all-start.5 = ((bf16[128,2,512]{2,1,0:T(2,128)(2,1)}), bf16[128,2,512]{2,1,0:T(2,128)(2,1)}, u32[]{:S(2)}, u32[]{:S(2)}) async-start(bf16[128,2,512]{2,1,0:T(2,128)(2,1)} %reshape.398), calls=%async_computation.5 | async-start | bytes 524288 | tf_op jit(solution)/shard_map/all_to_all | solution.py:95
  123.4 15.5 %all-to-all-start.6 = ((bf16[128,8,128]{2,1,0:T(8,128)(2,1)}), bf16[128,8,128]{2,1,0:T(8,128)(2,1)S(1)}, u32[]{:S(2)}, u32[]{:S(2)}) async-start(bf16[128,8,128]{2,1,0:T(8,128)(2,1)} %bitcast.23), calls=%async_computation.6 | async-start | bytes 524288 | tf_op jit(solution)/shard_map/all_to_all | solution.py:96
where the time goes:
time: 142 us
  waiting for transfers between devices  46.8 us (33%)
  starting transfers between devices  39.6 us (28%)
  matrix products  20.5 us (14%)
  blocking collectives  15 us (11%)
  other arithmetic  9 us (6%)
  local copies, waits for them, and re-layouts  8.09 us (6%)
  between operations  2.65 us (2%)
    dot_general x17, matrix products, dot(): lax.dot_general(a, b, (((ca,), (cb,)), ((), ())), preferred_element_type=...  20.5 us
    all_gather x1, blocking collectives, shards(): q_all = lax.all_gather(query_embed[0], 'group', axis=0, tiled=True)  15 us
    all_to_all x1, waiting for transfers between devices, shards(): lax.all_to_all(to_send, ('group', 'pair'), split_axis=0, concat_axis=0, t...  9.29 us
    all_to_all x1, waiting for transfers between devices, shards(): lax.all_to_all(values, ('group', 'pair'), split_axis=0, concat_axis=0, ti...  8.86 us
    all_to_all x1, waiting for transfers between devices, shards(): lax.all_to_all(req, ('group', 'pair'), split_axis=0, concat_axis=0, tiled...  8.3 us
    all_to_all x1, waiting for transfers between devices, shards(): lax.all_to_all(u_part.T, ('group', 'pair'), split_axis=0, concat_axis=0,...  7.87 us
    all_to_all x1, starting transfers between devices, shards(): lax.all_to_all(tags, 'pair', split_axis=0, concat_axis=0, tiled=True)  7.58 us
    all_to_all x1, waiting for transfers between devices, shards(): lax.all_to_all(u_part, ('group', 'pair'), split_axis=0, concat_axis=0, ti...  6.95 us
  transfers between devices with their start and end apart: 7, of which 6 were waited for; matrix products, arithmetic and copies ran while one was open for 12% of the time, Pallas kernels for 0%

commit v1 on v0

--- a/solution.py
+++ b/solution.py
@@ -6,6 +6,16 @@
 
 loss_scale = 1024.0
 f32, bf16, i32 = (jnp.float32, jnp.bfloat16, jnp.int32)
+
+
+def process_the_columns(packet):
+    return lax.all_to_all(
+        jnp.concatenate(tuple((packet for _ in range(lax.axis_size("group")))), 0),
+        axis_name="group",
+        split_axis=0,
+        concat_axis=0,
+        tiled=True,
+    )
 
 
 def iota(shape, dim):
@@ -50,7 +60,7 @@
     req = dot(owner_b, jnp.where(at_slot, high, 0).astype(bf16), 1, 1) * 256.0 + dot(
         owner_b, jnp.where(at_slot, low, 0).astype(bf16), 1, 1
     )
-    q_all = lax.all_gather(query_embed[0], "group", axis=0, tiled=True)
+    q_all = process_the_columns(query_embed[0])
     got = lax.all_to_all(req, ("group", "pair"), split_axis=0, concat_axis=0, tiled=True)
     packed = got.reshape(n_group, n_pair, slots).sum(1).reshape(1, n_group * slots).astype(i32)
     pq = dot(q_all, projection, 1, 1).astype(bf16)

time: 142 us -> 149 us (1.049)
  blocking collectives: 15 us -> 0 us
  local copies, waits for them, and re-layouts: 8.09 us -> 19.1 us
  waiting for transfers between devices: 46.8 us -> 53.4 us
  starting transfers between devices: 39.6 us -> 46 us
  matrix products: 20.5 us -> 17.9 us
    all_gather x1 -> x0, blocking collectives: 15 us -> none  [shards(): q_all = lax.all_gather(query_embed[0], 'group', axis=0, tiled=True)]
    unnamed x9 -> x14, local copies, waits for them, and re-layouts: 5.06 us -> 14.7 us
    all_to_all x0 -> x1, waiting for transfers between devices: none -> 6.48 us  [process_the_columns(): lax.all_to_all(jnp.concatenate(tuple((packet for _ in range(lax.axis_size...]
    all_to_all x0 -> x1, starting transfers between devices: none -> 4.26 us  [process_the_columns(): lax.all_to_all(jnp.concatenate(tuple((packet for _ in range(lax.axis_size...]
    dot_general x17, matrix products: 20.5 us -> 17.9 us  [dot(): lax.dot_general(a, b, (((ca,), (cb,)), ((), ())), preferred_element_type=...]
    all_to_all x1, starting transfers between devices: 6.53 us -> 8.81 us  [shards(): lax.all_to_all(req, ('group', 'pair'), split_axis=0, concat_axis=0, tiled...]
  transfers between devices with their start and end apart: 7 -> 8, of which waited for: 6 -> 7; matrix products, arithmetic and copies ran while one was open for 12% -> 15% of each run, Pallas kernels for 0% -> 0%
where the time goes in v1:
time: 149 us; the launch traced here: 148 us
  waiting for transfers between devices  53.4 us (36%)
  starting transfers between devices  46 us (31%)
  local copies, waits for them, and re-layouts  19.1 us (13%)
  matrix products  17.9 us (12%)
  other arithmetic  9 us (6%)
  between operations  2.66 us (2%)
    dot_general x17, matrix products, dot(): lax.dot_general(a, b, (((ca,), (cb,)), ((), ())), preferred_element_type=...  17.9 us
    unnamed x14, local copies, waits for them, and re-layouts  14.7 us
    all_to_all x1, waiting for transfers between devices, shards(): lax.all_to_all(to_send, ('group', 'pair'), split_axis=0, concat_axis=0, t...  9.42 us
    all_to_all x1, waiting for transfers between devices, shards(): lax.all_to_all(values, ('group', 'pair'), split_axis=0, concat_axis=0, ti...  8.86 us
    all_to_all x1, starting transfers between devices, shards(): lax.all_to_all(req, ('group', 'pair'), split_axis=0, concat_axis=0, tiled...  8.81 us
    all_to_all x1, waiting for transfers between devices, shards(): lax.all_to_all(req, ('group', 'pair'), split_axis=0, concat_axis=0, tiled...  8.3 us
    all_to_all x1, waiting for transfers between devices, shards(): lax.all_to_all(u_part.T, ('group', 'pair'), split_axis=0, concat_axis=0,...  7.87 us
    all_to_all x1, starting transfers between devices, shards(): lax.all_to_all(tags, 'pair', split_axis=0, concat_axis=0, tiled=True)  7.58 us
  transfers between devices with their start and end apart: 8, of which 7 were waited for; matrix products, arithmetic and copies ran while one was open for 15% of the time, Pallas kernels for 0%

profile of v1, /device:TPU:1, one launch (start us, length us, event | category | flops | bytes accessed | tf_op | source)
XLA Modules:
  0.0 148.0 jit_solution(9280655798290494427)
XLA Ops:
  4.4 7.6 %all-to-all-start = ((s32[16,1,32]{2,1,0:T(1,128)}), s32[16,1,32]{2,1,0:T(1,128)S(1)}, u32[]{:S(2)}, u32[]{:S(2)}) async-start(s32[16,1,32]{2,1,0:T(1,128)} %add.119), calls=%async_computation | async-start | bytes 16384 | tf_op jit(solution)/shard_map/all_to_all | solution.py:78
  12.9 1.4 bitcast_dynamic-update-slice_fusion.6
  24.9 6.7 %all-to-all-start.4 = ((f32[16,1,32]{2,1,0:T(1,128)}), f32[16,1,32]{2,1,0:T(1,128)S(1)}, u32[]{:S(2)}, u32[]{:S(2)}) async-start(f32[16,1,32]{2,1,0:T(1,128)} %bitcast.79), calls=%async_computation.4 | async-start | bytes 16384 | tf_op jit(solution)/shard_map/all_to_all | solution.py:79
  32.4 5.6 %all-to-all-done.4 = f32[16,1,32]{2,1,0:T(1,128)S(1)} async-done(((f32[16,1,32]{2,1,0:T(1,128)}), f32[16,1,32]{2,1,0:T(1,128)S(1)}, u32[]{:S(2)}, u32[]{:S(2)}) %all-to-all-start.4) | async-done | bytes 2080 | tf_op jit(solution)/shard_map/all_to_all | solution.py:79
  37.9 8.8 %all-to-all-start.1 = ((f32[128,1,128]{2,1,0:T(1,128)}), f32[128,1,128]{2,1,0:T(1,128)S(1)}, u32[]{:S(2)}, u32[]{:S(2)}) async-start(f32[128,1,128]{2,1,0:T(1,128)} %bitcast.3), calls=%async_computation.1 | async-start | bytes 131072 | tf_op jit(solution)/shard_map/all_to_all | solution.py:64
  48.0 8.3 %all-to-all-done.1 = f32[128,1,128]{2,1,0:T(1,128)S(1)} async-done(((f32[128,1,128]{2,1,0:T(1,128)}), f32[128,1,128]{2,1,0:T(1,128)S(1)}, u32[]{:S(2)}, u32[]{:S(2)}) %all-to-all-start.1) | async-done | bytes 65568 | tf_op jit(solution)/shard_map/all_to_all | solution.py:64
  56.3 4.3 %all-to-all-start.2 = ((bf16[8,16,1024]{2,1,0:T(8,128)(2,1)}), bf16[8,16,1024]{2,1,0:T(8,128)(2,1)S(1)}, u32[]{:S(2)}, u32[]{:S(2)}) async-start(bf16[8,16,1024]{2,1,0:T(8,128)(2,1)} %bitcast.7), calls=%async_computation.2 | async-start | bytes 524288 | tf_op jit(solution)/shard_map/all_to_all | solution.py:12
  60.6 6.5 %all-to-all-done.2 = bf16[8,16,1024]{2,1,0:T(8,128)(2,1)S(1)} async-done(((bf16[8,16,1024]{2,1,0:T(8,128)(2,1)}), bf16[8,16,1024]{2,1,0:T(8,128)(2,1)S(1)}, u32[]{:S(2)}, u32[]{:S(2)}) %all-to-all-start.2) | async-done | bytes 262176 | tf_op jit(solution)/shard_map/all_to_all | solution.py:12
  67.9 3.7 %convolution_multiply_fusion = f32[128,2048]{1,0:T(8,128)S(1)} fusion(bf16[128,1024]{1,0:T(8,128)(2,1)S(1)} %convolution_convert_fusion, bf16[2048,1024]{1,0:T(8,128)(2,1)} %param.10), kind=kOutput, calls=%fused_computation.8 | convolution fusion | flops 537133056 | bytes 5505024 | tf_op jit(solution)/shard_map/dot_general | solution.py:26
  71.6 1.7 %fusion.1 = f32[128,1024]{1,0:T(8,128)S(1)} fusion(s32[1024]{0:T(1024)S(1)} %add_bitcast_fusion, f32[128,2048]{1,0:T(8,128)S(1)} %convolution_multiply_fusion), kind=kOutput, calls=%fused_computation.3 | convolution fusion | flops 540016640 | bytes 1576960 | tf_op jit(solution)/shard_map/dot_general | solution.py:26
  73.4 1.8 %fusion.9 = f32[1024]{0:T(1024)S(1)} fusion(f32[128,1024]{1,0:T(8,128)S(1)} %fusion.1, s32[1024]{0:T(1024)S(1)} %add_bitcast_fusion, f32[128,2048]{1,0:T(8,128)S(1)} %convolution_multiply_fusion, s32[1024]{0:T(1024)S(1)} %bitcast_add_fusion), kind=kOutput, calls=%fused_computation.15 | convolution fusion | flops 539753472 | bytes 1585152 | tf_op jit(solution)/shard_map/dot_general | solution.py:26
  75.8 4.4 %all-to-all-start.3 = ((f32[128,1,128]{2,1,0:T(1,128)}), f32[128,1,128]{2,1,0:T(1,128)S(1)}, u32[]{:S(2)}, u32[]{:S(2)}) async-start(f32[128,1,128]{2,1,0:T(1,128)} %bitcast.11), calls=%async_computation.3 | async-start | bytes 131072 | tf_op jit(solution)/shard_map/all_to_all | solution.py:76
  80.4 9.4 %all-to-all-done.3 = f32[128,1,128]{2,1,0:T(1,128)S(1)} async-done(((f32[128,1,128]{2,1,0:T(1,128)}), f32[128,1,128]{2,1,0:T(1,128)S(1)}, u32[]{:S(2)}, u32[]{:S(2)}) %all-to-all-start.3) | async-done | bytes 65568 | tf_op jit(solution)/shard_map/all_to_all | solution.py:76
  92.3 4.5 %all-to-all-start.5 = ((f32[128,1,128]{2,1,0:T(1,128)}), f32[128,1,128]{2,1,0:T(1,128)S(1)}, u32[]{:S(2)}, u32[]{:S(2)}) async-start(f32[128,1,128]{2,1,0:T(1,128)} %bitcast.18), calls=%async_computation.5 | async-start | bytes 131072 | tf_op jit(solution)/shard_map/all_to_all | solution.py:96
  97.5 8.9 %all-to-all-done.5 = f32[128,1,128]{2,1,0:T(1,128)S(1)} async-done(((f32[128,1,128]{2,1,0:T(1,128)}), f32[128,1,128]{2,1,0:T(1,128)S(1)}, u32[]{:S(2)}, u32[]{:S(2)}) %all-to-all-start.5) | async-done | bytes 65568 | tf_op jit(solution)/shard_map/all_to_all | solution.py:96
  106.3 1.6 %fusion.6 = bf16[2048,128]{1,0:T(8,128)(2,1)S(1)} fusion(s32[1024]{0:T(1024)S(1)} %add_bitcast_fusion, bf16[16,8,8,128]{3,2,1,0:T(8,128)(2,1)S(1)} %bitcast.72, s32[1024]{0:T(1024)S(1)} %get-tuple-element.14, s32[1024]{0:T(1024)S(1)} %get-tuple-element.15, s32[128]{0:T(128)S(1)} %get-tuple-element.16, s32[128]{0:T(128)S(1)} %get-tuple-element.17, ...), kind=kOutput, calls=%fused_computation.9 | convolution fusion | flops 539754496 | bytes 800896 | tf_op jit(solution)/shard_map/dot_general | solution.py:26
  109.8 1.5 reduce.14
  111.2 1.8 %reshape.399 = bf16[128,2,512]{2,1,0:T(2,128)(2,1)} reshape(bf16[128,1024]{1,0:T(8,128)(2,1)} %reduce.14) | data formatting | bytes 524288
  113.1 5.6 %all-to-all-start.6 = ((bf16[128,2,512]{2,1,0:T(2,128)(2,1)}), bf16[128,2,512]{2,1,0:T(2,128)(2,1)}, u32[]{:S(2)}, u32[]{:S(2)}) async-start(bf16[128,2,512]{2,1,0:T(2,128)(2,1)} %reshape.399), calls=%async_computation.6 | async-start | bytes 524288 | tf_op jit(solution)/shard_map/all_to_all | solution.py:105
  119.5 3.3 %multiply_convert_fusion = bf16[2048,1024]{1,0:T(8,128)(2,1)} fusion(bf16[2048,128]{1,0:T(8,128)(2,1)S(1)} %fusion.6, bf16[128,1024]{1,0:T(8,128)(2,1)S(1)} %convolution_convert_fusion), kind=kOutput, calls=%fused_computation | convolution fusion | flops 541065216 | bytes 4980736 | tf_op jit(solution)/shard_map/dot_general | solution.py:26
  122.8 7.0 %all-to-all-done.6 = bf16[128,2,512]{2,1,0:T(2,128)(2,1)} async-done(((bf16[128,2,512]{2,1,0:T(2,128)(2,1)}), bf16[128,2,512]{2,1,0:T(2,128)(2,1)}, u32[]{:S(2)}, u32[]{:S(2)}) %all-to-all-start.6) | async-done | bytes 262176 | tf_op jit(solution)/shard_map/all_to_all | solution.py:105
  129.7 4.2 %all-to-all-start.7 = ((bf16[128,8,128]{2,1,0:T(8,128)(2,1)}), bf16[128,8,128]{2,1,0:T(8,128)(2,1)S(1)}, u32[]{:S(2)}, u32[]{:S(2)}) async-start(bf16[128,8,128]{2,1,0:T(8,128)(2,1)} %bitcast.25), calls=%async_computation.7 | async-start | bytes 524288 | tf_op jit(solution)/shard_map/all_to_all | solution.py:106
  133.9 2.2 %reshape.400 = bf16[128,1,1024]{2,1,0:T(2,128)(2,1)S(1)} reshape(bf16[128,2,512]{2,1,0:T(2,128)(2,1)} %all-to-all-done.6) | data formatting | bytes 524288
  137.4 7.9 %all-to-all-done.7 = bf16[128,8,128]{2,1,0:T(8,128)(2,1)S(1)} async-done(((bf16[128,8,128]{2,1,0:T(8,128)(2,1)}), bf16[128,8,128]{2,1,0:T(8,128)(2,1)S(1)}, u32[]{:S(2)}, u32[]{:S(2)}) %all-to-all-start.7) | async-done | bytes 262176 | tf_op jit(solution)/shard_map/all_to_all | solution.py:106
  (63 shorter events, 27.1 us)
Async XLA Ops:
  0.6 66.5 %copy-start = (bf16[1024,1024]{1,0:T(8,128)(2,1)S(1)}, bf16[1024,1024]{1,0:T(8,128)(2,1)}, u32[]{:S(2)}) copy-start(bf16[1024,1024]{1,0:T(8,128)(2,1)} %param.11) | copy-start | bytes 6291460
  4.4 20.5 %all-to-all-start = ((s32[16,1,32]{2,1,0:T(1,128)}), s32[16,1,32]{2,1,0:T(1,128)S(1)}, u32[]{:S(2)}, u32[]{:S(2)}) async-start(s32[16,1,32]{2,1,0:T(1,128)} %add.119), calls=%async_computation | async-start | bytes 16384 | tf_op jit(solution)/shard_map/all_to_all | solution.py:78
  24.9 13.0 %all-to-all-start.4 = ((f32[16,1,32]{2,1,0:T(1,128)}), f32[16,1,32]{2,1,0:T(1,128)S(1)}, u32[]{:S(2)}, u32[]{:S(2)}) async-start(f32[16,1,32]{2,1,0:T(1,128)} %bitcast.79), calls=%async_computation.4 | async-start | bytes 16384 | tf_op jit(solution)/shard_map/all_to_all | solution.py:79
  37.9 18.4 %all-to-all-start.1 = ((f32[128,1,128]{2,1,0:T(1,128)}), f32[128,1,128]{2,1,0:T(1,128)S(1)}, u32[]{:S(2)}, u32[]{:S(2)}) async-start(f32[128,1,128]{2,1,0:T(1,128)} %bitcast.3), calls=%async_computation.1 | async-start | bytes 131072 | tf_op jit(solution)/shard_map/all_to_all | solution.py:64
  56.3 10.8 %all-to-all-start.2 = ((bf16[8,16,1024]{2,1,0:T(8,128)(2,1)}), bf16[8,16,1024]{2,1,0:T(8,128)(2,1)S(1)}, u32[]{:S(2)}, u32[]{:S(2)}) async-start(bf16[8,16,1024]{2,1,0:T(8,128)(2,1)} %bitcast.7), calls=%async_computation.2 | async-start | bytes 524288 | tf_op jit(solution)/shard_map/all_to_all | solution.py:12
  75.8 14.1 %all-to-all-start.3 = ((f32[128,1,128]{2,1,0:T(1,128)}), f32[128,1,128]{2,1,0:T(1,128)S(1)}, u32[]{:S(2)}, u32[]{:S(2)}) async-start(f32[128,1,128]{2,1,0:T(1,128)} %bitcast.11), calls=%async_computation.3 | async-start | bytes 131072 | tf_op jit(solution)/shard_map/all_to_all | solution.py:76
  92.3 14.0 %all-to-all-start.5 = ((f32[128,1,128]{2,1,0:T(1,128)}), f32[128,1,128]{2,1,0:T(1,128)S(1)}, u32[]{:S(2)}, u32[]{:S(2)}) async-start(f32[128,1,128]{2,1,0:T(1,128)} %bitcast.18), calls=%async_computation.5 | async-start | bytes 131072 | tf_op jit(solution)/shard_map/all_to_all | solution.py:96
  106.3 2.2 %copy-start.1 = (bf16[2048,1024]{1,0:T(8,128)(2,1)S(1)}, bf16[2048,1024]{1,0:T(8,128)(2,1)}, u32[]{:S(2)}) copy-start(bf16[2048,1024]{1,0:T(8,128)(2,1)} %param.10) | copy-start | bytes 12582916
  113.1 16.7 %all-to-all-start.6 = ((bf16[128,2,512]{2,1,0:T(2,128)(2,1)}), bf16[128,2,512]{2,1,0:T(2,128)(2,1)}, u32[]{:S(2)}, u32[]{:S(2)}) async-start(bf16[128,2,512]{2,1,0:T(2,128)(2,1)} %reshape.399), calls=%async_computation.6 | async-start | bytes 524288 | tf_op jit(solution)/shard_map/all_to_all | solution.py:105
  129.7 15.5 %all-to-all-start.7 = ((bf16[128,8,128]{2,1,0:T(8,128)(2,1)}), bf16[128,8,128]{2,1,0:T(8,128)(2,1)S(1)}, u32[]{:S(2)}, u32[]{:S(2)}) async-start(bf16[128,8,128]{2,1,0:T(8,128)(2,1)} %bitcast.25), calls=%async_computation.7 | async-start | bytes 524288 | tf_op jit(solution)/shard_map/all_to_all | solution.py:106
